TPU v7x, 256 devices: a whole 4x4x8 slice. The times are simulated.
256 devices in a mesh: tm: 8 (over z_lo, core), chan: 32 (over z_hi, y, x).
Axes of the slice: x: 4, y: 4, z: 8 (z_hi: 2, z_lo: 4; z = z_hi * 4 + z_lo), core: 2. Of those that a mesh axis runs over, the one named last changes fastest.
Arguments:
- raw_strain: bfloat16 [256000, 4096], P('tm', 'chan'), may hold values from -600 to 600
- source_blocks: int32 [2], replicated, may hold values from 0 to 27, as said below
- band_bins: int32 [2], replicated, may hold values from 0 to 20, as said below
Outputs:
- cross_spectra: bfloat16 [1280, 2, 20, 4096], P('tm', None, None, 'chan')
Inputs may be any that keep to these rules, and one draw needn't show every extreme that they name: `source_blocks`: each entry is the index of the channel block of 128 channels at which a virtual-source block of 640 channels begins; the two entries differ, one of them is always the last possible start, and the blocks may intersect. band_bins[0] is at most 2 and band_bins[1] is at least 18.
All inputs are finite; a program needn't handle non-finite values.
Results may differ from a plain program's by a relative error of at most 0.0091.
Values may be sent and summed in bfloat16 or wider, within the bound.
A program may use at most 64 MiB of HBM per device.

v0:
```python
import math
import jax
import jax.numpy as jnp
import numpy as np
from jax import lax
from jax.sharding import PartitionSpec as P

NW = 16
WIN = 500
NB = 20
VS = 640
TAPS = 64
DECIM = 4


def from_behind(value, axis, steps):
    count = lax.axis_size(axis)
    initial, last = (max(0, -steps), min(count, count - steps))
    return lax.ppermute(value, axis, [(source, source + steps) for source in range(initial, last)])


def carried_in(part, axis, combine, identity):
    place = lax.axis_index(axis)
    gathered = jax.tree.map(lambda a: lax.all_gather(a, axis), part)
    state = jax.tree.map(lambda a, e: jnp.zeros_like(a) + jnp.asarray(e, a.dtype), part, identity)

    def one(step, state):
        return combine(
            state, jax.tree.map(lambda a: lax.dynamic_index_in_dim(a, step, 0, False), gathered)
        )

    return lax.fori_loop(0, place, one, state)


def lowpass_taps():
    offsets = np.arange(TAPS) - (TAPS - 1) / 2.0
    window = 0.54 - 0.46 * np.cos(2.0 * np.pi * np.arange(TAPS) / (TAPS - 1))
    angles = np.pi * 0.8 * offsets / DECIM
    values = np.sin(angles) / angles * window
    return values / values.sum()


def filter_tables():
    tap_values = lowpass_taps()
    carried = TAPS - DECIM
    outputs = np.arange(WIN)[:, None]
    inputs = np.arange(DECIM * WIN)[None, :]
    lag_main = DECIM * outputs + DECIM - 1 - inputs
    main_table = np.where(
        (lag_main >= 0) & (lag_main < TAPS), tap_values[np.clip(lag_main, 0, TAPS - 1)], 0.0
    )
    earlier_ids = np.arange(carried)[None, :]
    lag_edge = DECIM * outputs + DECIM - 1 - (earlier_ids - carried)
    edge_table = np.where(
        (lag_edge >= 0) & (lag_edge < TAPS), tap_values[np.clip(lag_edge, 0, TAPS - 1)], 0.0
    )
    return (jnp.asarray(main_table, jnp.bfloat16), jnp.asarray(edge_table, jnp.bfloat16))


def running_tables():
    forget = math.exp(-1.0 / WIN)
    step_ids = np.arange(WIN)
    step_gaps = step_ids[:, None] - step_ids[None, :]
    within = np.where(step_gaps >= 0, (1.0 - forget) * forget ** np.maximum(step_gaps, 0), 0.0)
    window_ids = np.arange(NW)
    lag_table = np.arange(NW + 1)[:, None] - 1 - window_ids[None, :]
    carry_table = np.where(lag_table >= 0, forget ** (WIN * np.maximum(lag_table, 0)), 0.0)
    window_powers = forget ** (WIN * window_ids)
    rising = forget ** (step_ids + 1.0)
    return (
        jnp.asarray(within, jnp.float32),
        jnp.asarray(carry_table, jnp.float32),
        jnp.asarray(window_powers, jnp.float32),
        jnp.asarray(rising, jnp.float32),
    )


def spectrum_table():
    time_ids = np.arange(WIN)
    freq_ids = np.arange(1, NB + 1)
    phases = 2.0 * np.pi * freq_ids[:, None] * time_ids[None, :] / WIN
    return jnp.asarray(
        np.concatenate([np.cos(phases), -np.sin(phases)], axis=0) / np.sqrt(WIN), jnp.bfloat16
    )


def gather_groups(whitened):
    return lax.all_gather(whitened[None], "tm", axis=0, tiled=True)


def body(raw_strain, source_blocks, band_bins):
    channels_here = raw_strain.shape[1]
    carried = TAPS - DECIM
    raw_window = DECIM * WIN
    windows = raw_strain.reshape(NW, raw_window, channels_here)
    main_table, edge_table = filter_tables()
    previous = from_behind(raw_strain[NW * raw_window - carried :], "tm", 1)
    earlier = jnp.concatenate([previous[None], windows[: NW - 1, raw_window - carried :]], axis=0)
    decimated = jnp.einsum("mr,wrc->wmc", main_table, windows, preferred_element_type=jnp.float32)
    decimated = decimated + jnp.einsum(
        "mq,wqc->wmc", edge_table, earlier, preferred_element_type=jnp.float32
    )
    within, carry_table, window_powers, rising = running_tables()
    energy = decimated * decimated
    local_run = jnp.einsum("tu,wuc->wtc", within, energy, precision=lax.Precision.HIGHEST)
    window_ends = local_run[:, WIN - 1, :]
    entering = jnp.dot(carry_table, window_ends, precision=lax.Precision.HIGHEST)
    block_total = entering[NW]

    def compose(earlier_map, later_map):
        return (earlier_map[0] * later_map[0], later_map[0] * earlier_map[1] + later_map[1])

    factors = jnp.full((channels_here,), math.exp(-NW), jnp.float32)
    prefix_maps = carried_in(
        (factors, block_total), "tm", compose, (jnp.ones_like(factors), jnp.zeros_like(block_total))
    )
    incoming = prefix_maps[1]
    starts = entering[:NW] + window_powers[:, None] * incoming[None, :]
    running = local_run + rising[None, :, None] * starts[:, None, :]
    normalized = (decimated / jnp.sqrt(jnp.maximum(running, 0.01))).astype(jnp.bfloat16)
    spectra = jnp.einsum(
        "kt,wtc->wkc", spectrum_table(), normalized, preferred_element_type=jnp.float32
    )
    band_power = jnp.sum(spectra * spectra, axis=1) / NB
    bin_index = jnp.arange(NB)
    band_keep = ((bin_index >= band_bins[0]) & (bin_index < band_bins[1])).astype(jnp.float32)
    band_keep = jnp.concatenate([band_keep, band_keep])
    whitened = (
        spectra * band_keep[None, :, None] / jnp.sqrt(jnp.maximum(band_power, 0.1))[:, None, :]
    ).astype(jnp.bfloat16)
    groups = lax.axis_size("tm")
    src_share = 2 * VS // groups
    own_all = gather_groups(whitened)
    gathered = lax.all_gather(whitened, "chan", axis=2, tiled=True)
    first_block = lax.dynamic_slice_in_dim(gathered, source_blocks[0] * channels_here, VS, 2)
    second_block = lax.dynamic_slice_in_dim(gathered, source_blocks[1] * channels_here, VS, 2)
    picked = jnp.concatenate([first_block, second_block], axis=2)
    shares = lax.all_to_all(picked[None], "tm", split_axis=3, concat_axis=0, tiled=True)
    own_spectra = own_all.reshape(groups, NW, 2, NB, channels_here)
    source_groups = shares.reshape(groups, NW, 2, NB, src_share)
    rotated = jnp.stack([-source_groups[:, :, 1], source_groups[:, :, 0]], axis=2)
    turned = jnp.stack([source_groups, rotated], axis=3)
    stack_scale = 1.0 / math.sqrt(groups * NW)

    def add_group(group_index, stacked_sum):
        own_block = lax.dynamic_index_in_dim(own_spectra, group_index, 0, False)
        src_block = lax.dynamic_index_in_dim(turned, group_index, 0, False)
        group_term = (
            jnp.einsum("wpkc,wpqks->sqkc", own_block, src_block, preferred_element_type=jnp.float32)
            * stack_scale
        )
        return stacked_sum + lax.optimization_barrier(group_term.astype(jnp.bfloat16)).astype(
            jnp.float32
        )

    stacked_sum = lax.fori_loop(
        0, groups, add_group, jnp.zeros((src_share, 2, NB, channels_here), jnp.float32)
    )
    return stacked_sum.astype(jnp.bfloat16)


def solution(mesh):
    in_specs = (P("tm", "chan"), P(), P())
    out_specs = P("tm", None, None, "chan")
    return jax.shard_map(body, mesh=mesh, in_specs=in_specs, out_specs=out_specs, check_vma=False)
```

profile of v0, /device:TPU:1, one launch (start us, length us, event | category | flops | bytes accessed | tf_op | source)
XLA Modules:
  0.0 365.0 jit_solution(10536839834026932320)
XLA Ops:
  7.4 0.7 slice.33
  8.1 4.9 %collective-permute-start = (bf16[60,128]{1,0:T(8,128)(2,1)S(1)}, bf16[60,128]{1,0:T(8,128)(2,1)S(1)}, u32[]{:S(2)}, u32[]{:S(2)}) collective-permute-start(bf16[60,128]{1,0:T(8,128)(2,1)S(1)} %slice.33), channel_id=1, source_target_pairs={{0,32},{32,64},{64,96},{96,128},{128,160},{160,192},{192,224},{1,3... | collective-permute-start | bytes 46088 | tf_op jit(solution)/shard_map/ppermute | solution.py:19
  13.0 1.3 fusion.14
  14.4 10.4 %fusion.15 = f32[500,16,128]{2,0,1:T(8,128)} fusion(bf16[500,2000,1]{0,1,2:T(8,128)(2,1)} %constant.102, bf16[16,2000,128]{2,1,0:T(8,128)(2,1)} %bitcast.88), kind=kOutput, calls=%fused_computation.37 | convolution fusion | flops 4096000000 | bytes 14288000 | tf_op jit(solution)/shard_map/mr,wrc->wmc/dot_general | solution.py:99
  24.8 1.3 compare_and_fusion
  26.1 0.1 add_convert_fusion
  26.1 1.0 slice.44
  27.2 0.0 collective-permute-done
  27.2 0.0 copy-start.2
  27.2 3.0 bitcast_add_fusion.1
  30.2 0.0 copy-done.2
  30.2 0.0 copy-start
  30.2 0.0 copy-start.5
  30.2 0.0 copy-start.8
  30.2 0.0 copy-start.4
  30.3 0.0 copy-start.7
  30.3 7.4 %fusion.4 = f32[16,500,128]{2,1,0:T(8,128)S(1)} fusion(f32[500,500,1]{1,0,2:T(8,128)S(1)} %copy-done.2, f32[16,128,500]{1,2,0:T(8,128)S(1)} %bitcast_add_fusion.1), kind=kOutput, calls=%fused_computation.16 | convolution fusion | flops 6145024000 | bytes 9192000 | tf_op jit(solution)/shard_map/tu,wuc->wtc/dot_general | solution.py:105
  37.7 0.0 copy-done
  37.7 0.0 copy-start.1
  37.7 1.9 copy-done.1
  39.7 0.1 fusion.16
  39.8 11.2 %all-gather.1 = f32[8,1,128]{2,1,0:T(1,128)S(1)} all-gather(f32[1,1,128]{2,1,0:T(1,128)S(1)} %slice_bitcast_fusion), channel_id=1, replica_groups=mesh['tm'=8,'chan'=32] {'tm'}, dimensions={0}, use_global_device_ids=true | all-gather | bytes 4608 | tf_op jit(solution)/shard_map/all_gather | solution.py:24
  51.1 0.2 while.27
  51.3 0.0 copy-done.8
  51.3 0.1 slice_add_fusion
  51.4 4.4 %multiply_reduce_fusion = (f32[16,128]{1,0:T(8,128)S(1)}, f32[16,128,40]{1,2,0:T(8,128)S(1)}) fusion(bf16[40,500,1]{1,0,2:T(8,128)(2,1)S(1)} %copy-done.4, f32[16,128,500]{1,2,0:T(8,128)} %copy-done, f32[16,500,128]{2,1,0:T(8,128)} %copy-done.1, f32[16,128]{1,0:T(8,128)S(1)} %slice_add_fusion, f32[500]{0:T(512)S(1)} %copy-done.7), kind=kOutput, calls=%fused_computation.21 | convolution fusion | flops 87201792 | bytes 8578064 | tf_op jit(solution)/shard_map/kt,wtc->wkc/dot_general | solution.py:121
  55.8 0.8 fusion.10
  56.6 0.0 all-gather.5.cloned.1.call-update
  56.6 0.6 fusion.13
  58.5 149.2 %all-gather.5.cloned.1.call-done = bf16[16,40,4096]{2,1,0:T(8,128)(2,1)} async-done(((bf16[16,40,128]{2,1,0:T(8,128)(2,1)}), bf16[16,40,4096]{2,1,0:T(8,128)(2,1)}) %all-gather.5.cloned.1.call-update) | async-done | bytes 5242896 | tf_op jit(solution)/shard_map/all_gather | solution.py:134
  207.7 1.5 constant_dynamic-slice_fusion.3
  209.2 0.1 maximum_bitcast_fusion.1
  209.4 5.7 %copy.23 = bf16[1,16,40,1280]{2,1,0,3:T(8,128)(2,1)} copy(bf16[1,16,40,1280]{3,2,1,0:T(8,128)(2,1)S(1)} %maximum_bitcast_fusion.1) | data formatting | bytes 3276800 | tf_op jit(solution)/shard_map/broadcast_in_dim | solution.py:138
  215.1 10.2 %reshape.38 = bf16[8,2,51200]{2,1,0:T(2,128)(2,1)} reshape(bf16[1280,1,16,40]{3,2,1,0:T(8,128)(2,1)} %bitcast.81) | data formatting | bytes 3276800
  225.3 5.8 %all-to-all-start = ((bf16[8,2,51200]{2,1,0:T(2,128)(2,1)}), bf16[8,2,51200]{2,1,0:T(2,128)(2,1)}, u32[]{:S(2)}, u32[]{:S(2)}) async-start(bf16[8,2,51200]{2,1,0:T(2,128)(2,1)} %reshape.38), calls=%async_computation | async-start | bytes 3276800 | tf_op jit(solution)/shard_map/all_to_all | solution.py:138
  231.1 0.6 all-gather.7.cloned.1.call-update
  231.6 50.4 %all-gather.7.cloned.1.call-done = bf16[128,40,128]{2,1,0:T(8,128)(2,1)} async-done(((bf16[16,40,128]{2,1,0:T(8,128)(2,1)}), bf16[128,40,128]{2,1,0:T(8,128)(2,1)}) %all-gather.7.cloned.1.call-update) | async-done | bytes 1310736 | tf_op jit(solution)/shard_map/all_gather | solution.py:88
  282.0 2.8 copy.27
  284.8 0.0 all-to-all-done
  284.8 10.4 %reshape.39 = bf16[1280,1,16,40]{3,2,1,0:T(8,128)(2,1)} reshape(bf16[8,2,51200]{2,1,0:T(2,128)(2,1)} %all-to-all-done) | data formatting | bytes 3276800
  295.2 8.5 %copy.33 = bf16[1,16,40,8,160]{4,3,2,1,0:T(8,128)(2,1)} copy(bf16[1,16,40,8,160]{2,1,4,3,0:T(8,128)(2,1)} %bitcast.82) | data formatting | bytes 3276800 | tf_op jit(solution)/shard_map/all_to_all | solution.py:138
  303.7 3.2 copy.25
  307.0 0.2 slice_negate_fusion
  307.1 0.4 maximum_bitcast_fusion
  307.6 3.3 pad_maximum_fusion
  310.9 43.9 %while.28 = (s32[]{:T(128)}, f32[160,2,20,128]{3,0,1,2:T(8,128)S(1)}, bf16[8,16,2,2,20,160]{5,1,4,2,0,3:T(8,128)(2,1)}, bf16[8,16,2,20,128]{4,1,0,3,2:T(8,128)(2,1)}, s32[]{:T(128)}, /*index=5*/s32[]{:T(128)}) while((s32[]{:T(128)}, f32[160,2,20,128]{3,0,1,2:T(8,128)S(1)}, bf16[8,16,2,2,20,160]{5,1,4,2,0,3:T(8,128)(2,1)}, ...), condition=%wide.region_4.5_spmd.clone, body=%wide.region_3.4_spmd.clone.sunk | while | flops 56524800 | bytes 10650703 | solution.py:156
  310.9 3.0 fusion.25
  313.9 2.5 select_add_fusion.2
  316.4 3.0 fusion.25
  319.4 2.5 select_add_fusion.2
  321.9 3.0 fusion.25
  324.9 2.5 select_add_fusion.2
  327.4 3.0 fusion.25
  330.4 2.5 select_add_fusion.2
  332.9 3.0 fusion.25
  335.9 2.5 select_add_fusion.2
  338.4 3.0 fusion.25
  341.3 2.5 select_add_fusion.2
  343.9 3.0 fusion.25
  346.8 2.5 select_add_fusion.2
  349.4 3.0 fusion.25
  352.3 2.5 select_add_fusion.2
  354.8 0.3 convert_element_type.33
  355.1 2.4 copy.30
  (15 shorter events, 0.1 us)
Async XLA Ops:
  7.4 200.3 %all-gather.5.cloned.1.call-start = ((), (), s32[]{:S(2)}) async-start(), calls=%async_computation.1 | async-start | bytes 5406720 | tf_op jit(solution)/shard_map/all_gather | solution.py:134
  8.1 19.1 %collective-permute-start = (bf16[60,128]{1,0:T(8,128)(2,1)S(1)}, bf16[60,128]{1,0:T(8,128)(2,1)S(1)}, u32[]{:S(2)}, u32[]{:S(2)}) collective-permute-start(bf16[60,128]{1,0:T(8,128)(2,1)S(1)} %slice.33), channel_id=1, source_target_pairs={{0,32},{32,64},{64,96},{96,128},{128,160},{160,192},{192,224},{1,3... | collective-permute-start | bytes 46088 | tf_op jit(solution)/shard_map/ppermute | solution.py:19
  14.4 12.8 %copy-start.3 = (bf16[500,60,1]{0,1,2:T(8,128)(2,1)S(1)}, bf16[500,60,1]{0,1,2:T(8,128)(2,1)}, u32[]{:S(2)}) copy-start(bf16[500,60,1]{0,1,2:T(8,128)(2,1)} %constant.103) | copy-start | bytes 180004
  27.2 3.0 copy-start.2
  30.2 7.5 %copy-start = (f32[16,128,500]{1,2,0:T(8,128)}, f32[16,128,500]{1,2,0:T(8,128)S(1)}, u32[]{:S(2)}) copy-start(f32[16,128,500]{1,2,0:T(8,128)S(1)} %bitcast_add_fusion.1) | copy-start | bytes 12288004
  30.2 9.4 %copy-start.5 = (f32[17,16]{1,0:T(8,128)S(1)}, f32[17,16]{1,0:T(8,128)}, u32[]{:S(2)}) copy-start(f32[17,16]{1,0:T(8,128)} %constant.98.clone) | copy-start | bytes 3268
  30.2 21.0 %copy-start.8 = (f32[16]{0:T(128)S(1)}, f32[16]{0:T(128)}, u32[]{:S(2)}) copy-start(f32[16]{0:T(128)} %constant.99.clone) | copy-start | bytes 196
  30.2 21.1 %copy-start.4 = (bf16[40,500,1]{1,0,2:T(8,128)(2,1)S(1)}, bf16[40,500,1]{1,0,2:T(8,128)(2,1)}, u32[]{:S(2)}) copy-start(bf16[40,500,1]{1,0,2:T(8,128)(2,1)} %constant.105) | copy-start | bytes 120004
  30.3 21.1 %copy-start.7 = (f32[500]{0:T(512)S(1)}, f32[500]{0:T(512)}, u32[]{:S(2)}) copy-start(f32[500]{0:T(512)} %constant.100.clone) | copy-start | bytes 6004
  37.7 2.0 copy-start.1
  51.4 5.3 %copy-start.6 = (s32[2]{0:T(128)S(1)}, s32[2]{0:T(128)}, u32[]{:S(2)}) copy-start(s32[2]{0:T(128)} %param.15) | copy-start | bytes 28
  225.3 59.5 %all-to-all-start = ((bf16[8,2,51200]{2,1,0:T(2,128)(2,1)}), bf16[8,2,51200]{2,1,0:T(2,128)(2,1)}, u32[]{:S(2)}, u32[]{:S(2)}) async-start(bf16[8,2,51200]{2,1,0:T(2,128)(2,1)} %reshape.38), calls=%async_computation | async-start | bytes 3276800 | tf_op jit(solution)/shard_map/all_to_all | solution.py:138
  231.1 51.0 %all-gather.7.cloned.1.call-start = ((), (), s32[]{:S(2)}) async-start(), calls=%async_computation.2 | async-start | bytes 1474560 | tf_op jit(solution)/shard_map/all_gather | solution.py:88
Sparse Core Ops, SparseCore 0:
  56.7 150.9 all-gather.4
Sparse Core Ops, SparseCore 1:
  233.3 48.7 all-gather.6
where the time goes:
time: 366 us; the launch traced here: 365 us
  waiting for transfers between devices  200 us (55%)
  local copies, waits for them, and re-layouts  50.5 us (14%)
  matrix products  49.2 us (13%)
  other arithmetic  26.5 us (7%)
  between operations  16.4 us (4%)
  blocking collectives  11.2 us (3%)
  starting transfers between devices  10.7 us (3%)
    all_gather x1, waiting for transfers between devices, body(): gathered = lax.all_gather(whitened, 'chan', axis=2, tiled=True)  149 us
    all_gather x1, waiting for transfers between devices, gather_groups(): return lax.all_gather(whitened[None], 'tm', axis=0, tiled=True)  50.4 us
    dot_general x8, matrix products, add_group(): jnp.einsum('wpkc,wpqks->sqkc', own_block, src_block, preferred_element_ty...  23.8 us
    unnamed x21, local copies, waits for them, and re-layouts  22.6 us
    add x8, other arithmetic, add_group(): stacked_sum + lax.optimization_barrier(group_term.astype(jnp.bfloat16)).a...  20 us
    all_to_all x2, local copies, waits for them, and re-layouts, body(): lax.all_to_all(picked[None], 'tm', split_axis=3, concat_axis=0, tiled=True)  11.7 us
    all_gather x1, blocking collectives, carried_in(): gathered = jax.tree.map(lambda a: lax.all_gather(a, axis), part)  11.2 us
    dot_general x1, matrix products, body(): jnp.einsum('mr,wrc->wmc', main_table, windows, preferred_element_type=jnp...  10.4 us
  transfers between devices with their start and end apart: 4, of which 2 were waited for; matrix products, arithmetic and copies ran while one was open for 5% of the time, Pallas kernels for 0%

commit v1 on v0

--- a/solution.py
+++ b/solution.py
@@ -135,7 +135,10 @@
     first_block = lax.dynamic_slice_in_dim(gathered, source_blocks[0] * channels_here, VS, 2)
     second_block = lax.dynamic_slice_in_dim(gathered, source_blocks[1] * channels_here, VS, 2)
     picked = jnp.concatenate([first_block, second_block], axis=2)
-    shares = lax.all_to_all(picked[None], "tm", split_axis=3, concat_axis=0, tiled=True)
+    shares = jnp.concatenate(
+        lax.all_to_all(jnp.stack(jnp.split(picked[None], lax.axis_size("tm"), axis=3)), "tm", 0, 0),
+        axis=0,
+    )
     own_spectra = own_all.reshape(groups, NW, 2, NB, channels_here)
     source_groups = shares.reshape(groups, NW, 2, NB, src_share)
     rotated = jnp.stack([-source_groups[:, :, 1], source_groups[:, :, 0]], axis=2)

time: 366 us -> 355 us (0.970)
  local copies, waits for them, and re-layouts: 50.5 us -> 21.5 us
  waiting for transfers between devices: 200 us -> 218 us
    all_to_all x1, waiting for transfers between devices: 0.01 us -> 18.3 us  [body(): lax.all_to_all(jnp.stack(jnp.split(picked[None], lax.axis_size('tm'), axi...]
    unnamed x21 -> x26, local copies, waits for them, and re-layouts: 22.6 us -> 7.96 us
    all_to_all x2 -> x1, local copies, waits for them, and re-layouts: 11.7 us -> 2.3 us  [body(): lax.all_to_all(jnp.stack(jnp.split(picked[None], lax.axis_size('tm'), axi...]
    broadcast_in_dim x1 -> x0, local copies, waits for them, and re-layouts: 5.72 us -> none  [body(): picked[None]]
  transfers between devices with their start and end apart: 4 -> 4, of which waited for: 2 -> 3; matrix products, arithmetic and copies ran while one was open for 5% -> 5% of each run, Pallas kernels for 0% -> 0%
where the time goes in v1:
time: 355 us; the launch traced here: 354 us
  waiting for transfers between devices  218 us (61%)
  matrix products  49.2 us (14%)
  other arithmetic  26.5 us (7%)
  local copies, waits for them, and re-layouts  21.5 us (6%)
  between operations  16.3 us (5%)
  blocking collectives  11.2 us (3%)
  starting transfers between devices  10.8 us (3%)
    all_gather x1, waiting for transfers between devices, body(): gathered = lax.all_gather(whitened, 'chan', axis=2, tiled=True)  149 us
    all_gather x1, waiting for transfers between devices, gather_groups(): return lax.all_gather(whitened[None], 'tm', axis=0, tiled=True)  50.3 us
    dot_general x8, matrix products, add_group(): jnp.einsum('wpkc,wpqks->sqkc', own_block, src_block, preferred_element_ty...  23.8 us
    add x8, other arithmetic, add_group(): stacked_sum + lax.optimization_barrier(group_term.astype(jnp.bfloat16)).a...  20 us
    all_to_all x1, waiting for transfers between devices, body(): lax.all_to_all(jnp.stack(jnp.split(picked[None], lax.axis_size('tm'), axi...  18.3 us
    all_gather x1, blocking collectives, carried_in(): gathered = jax.tree.map(lambda a: lax.all_gather(a, axis), part)  11.2 us
    dot_general x1, matrix products, body(): jnp.einsum('mr,wrc->wmc', main_table, windows, preferred_element_type=jnp...  10.4 us
    unnamed x26, local copies, waits for them, and re-layouts  7.96 us
  transfers between devices with their start and end apart: 4, of which 3 were waited for; matrix products, arithmetic and copies ran while one was open for 5% of the time, Pallas kernels for 0%

profile of v1, /device:TPU:1, one launch (start us, length us, event | category | flops | bytes accessed | tf_op | source)
XLA Modules:
  0.0 354.3 jit_solution(15364803383288666050)
XLA Ops:
  7.4 0.7 slice.33
  8.1 4.9 %collective-permute-start = (bf16[60,128]{1,0:T(8,128)(2,1)S(1)}, bf16[60,128]{1,0:T(8,128)(2,1)S(1)}, u32[]{:S(2)}, u32[]{:S(2)}) collective-permute-start(bf16[60,128]{1,0:T(8,128)(2,1)S(1)} %slice.33), channel_id=1, source_target_pairs={{0,32},{32,64},{64,96},{96,128},{128,160},{160,192},{192,224},{1,3... | collective-permute-start | bytes 46088 | tf_op jit(solution)/shard_map/ppermute | solution.py:19
  13.0 1.3 fusion.22
  14.4 10.4 %fusion.23 = f32[500,16,128]{2,0,1:T(8,128)} fusion(bf16[500,2000,1]{0,1,2:T(8,128)(2,1)} %constant.102, bf16[16,2000,128]{2,1,0:T(8,128)(2,1)} %bitcast.113), kind=kOutput, calls=%fused_computation.53 | convolution fusion | flops 4096000000 | bytes 14288000 | tf_op jit(solution)/shard_map/mr,wrc->wmc/dot_general | solution.py:99
  24.8 1.3 compare_and_fusion
  26.1 0.1 add_convert_fusion
  26.1 1.0 slice.44
  27.2 0.0 collective-permute-done
  27.2 0.0 copy-start.2
  27.2 3.0 bitcast_add_fusion.1
  30.2 0.0 copy-done.2
  30.2 0.0 copy-start.5
  30.2 0.0 copy-start.8
  30.2 0.0 copy-start.4
  30.3 0.0 copy-start.7
  30.3 7.4 %fusion.4 = f32[16,500,128]{2,1,0:T(8,128)S(1)} fusion(f32[500,500,1]{1,0,2:T(8,128)S(1)} %copy-done.2, f32[16,128,500]{1,2,0:T(8,128)S(1)} %bitcast_add_fusion.1), kind=kOutput, calls=%fused_computation.16 | convolution fusion | flops 6145024000 | bytes 9192000 | tf_op jit(solution)/shard_map/tu,wuc->wtc/dot_general | solution.py:105
  37.7 1.9 copy-done.1
  39.7 0.1 fusion.24
  39.8 11.2 %all-gather.1 = f32[8,1,128]{2,1,0:T(1,128)S(1)} all-gather(f32[1,1,128]{2,1,0:T(1,128)S(1)} %slice_bitcast_fusion.8), channel_id=1, replica_groups=mesh['tm'=8,'chan'=32] {'tm'}, dimensions={0}, use_global_device_ids=true | all-gather | bytes 4608 | tf_op jit(solution)/shard_map/all_gather | solution.py:24
  51.1 0.2 while.27
  51.3 0.1 slice_add_fusion
  51.4 4.4 %multiply_reduce_fusion = (f32[16,128]{1,0:T(8,128)S(1)}, f32[16,128,40]{1,2,0:T(8,128)S(1)}) fusion(bf16[40,500,1]{1,0,2:T(8,128)(2,1)S(1)} %copy-done.4, f32[16,128,500]{1,2,0:T(8,128)} %copy-done, f32[16,500,128]{2,1,0:T(8,128)} %copy-done.1, f32[16,128]{1,0:T(8,128)S(1)} %slice_add_fusion, f32[500]{0:T(512)S(1)} %copy-done.7), kind=kOutput, calls=%fused_computation.37 | convolution fusion | flops 87201792 | bytes 8578064 | tf_op jit(solution)/shard_map/kt,wtc->wkc/dot_general | solution.py:121
  55.8 0.8 fusion.18
  56.6 0.0 all-gather.5.cloned.1.call-update
  56.6 0.6 fusion.21
  58.4 149.3 %all-gather.5.cloned.1.call-done = bf16[16,40,4096]{2,1,0:T(8,128)(2,1)} async-done(((bf16[16,40,128]{2,1,0:T(8,128)(2,1)}), bf16[16,40,4096]{2,1,0:T(8,128)(2,1)}) %all-gather.5.cloned.1.call-update) | async-done | bytes 5242896 | tf_op jit(solution)/shard_map/all_gather | solution.py:134
  207.7 1.5 constant_dynamic-slice_fusion.3
  209.2 0.1 maximum_bitcast_fusion.1
  209.4 0.8 fusion.14
  210.1 0.9 fusion.13
  211.0 0.9 fusion.12
  211.9 0.9 fusion.11
  212.8 0.7 fusion.10
  213.6 0.9 fusion.9
  214.5 0.9 fusion.8
  215.4 0.9 fusion.7
  216.3 5.8 %all-to-all-start = ((bf16[8,1,16,40,160]{4,3,2,1,0:T(8,128)(2,1)}), bf16[8,1,16,40,160]{4,3,2,1,0:T(8,128)(2,1)}, u32[]{:S(2)}, u32[]{:S(2)}) async-start(bf16[8,1,16,40,160]{4,3,2,1,0:T(8,128)(2,1)} %fusion.7), calls=%async_computation | async-start | bytes 5242880 | tf_op jit(solution)/shard_map/all_to_all | solution.py:139
  222.1 0.6 all-gather.7.cloned.1.call-update
  222.7 50.3 %all-gather.7.cloned.1.call-done = bf16[128,40,128]{2,1,0:T(8,128)(2,1)} async-done(((bf16[16,40,128]{2,1,0:T(8,128)(2,1)}), bf16[128,40,128]{2,1,0:T(8,128)(2,1)}) %all-gather.7.cloned.1.call-update) | async-done | bytes 1310736 | tf_op jit(solution)/shard_map/all_gather | solution.py:88
  272.9 2.7 copy.24
  275.6 18.3 %all-to-all-done = bf16[8,1,16,40,160]{4,3,2,1,0:T(8,128)(2,1)} async-done(((bf16[8,1,16,40,160]{4,3,2,1,0:T(8,128)(2,1)}), bf16[8,1,16,40,160]{4,3,2,1,0:T(8,128)(2,1)}, u32[]{:S(2)}, u32[]{:S(2)}) %all-to-all-start) | async-done | bytes 1638432 | tf_op jit(solution)/shard_map/all_to_all | solution.py:139
  293.9 2.3 copy.22
  296.2 0.2 slice_negate_fusion
  296.4 0.4 maximum_bitcast_fusion
  296.9 3.3 pad_maximum_fusion
  300.2 43.9 %while.28 = (s32[]{:T(128)}, f32[160,2,20,128]{3,0,1,2:T(8,128)S(1)}, bf16[8,16,2,2,20,160]{5,1,4,2,0,3:T(8,128)(2,1)}, bf16[8,16,2,20,128]{4,1,0,3,2:T(8,128)(2,1)}, s32[]{:T(128)}, /*index=5*/s32[]{:T(128)}) while((s32[]{:T(128)}, f32[160,2,20,128]{3,0,1,2:T(8,128)S(1)}, bf16[8,16,2,2,20,160]{5,1,4,2,0,3:T(8,128)(2,1)}, ...), condition=%wide.region_4.5_spmd.clone, body=%wide.region_3.4_spmd.clone.sunk | while | flops 56524800 | bytes 10650703 | solution.py:159
  300.2 3.0 fusion.33
  303.2 2.5 select_add_fusion.2
  305.7 3.0 fusion.33
  308.7 2.5 select_add_fusion.2
  311.2 3.0 fusion.33
  314.2 2.5 select_add_fusion.2
  316.7 3.0 fusion.33
  319.7 2.5 select_add_fusion.2
  322.2 3.0 fusion.33
  325.1 2.5 select_add_fusion.2
  327.7 3.0 fusion.33
  330.6 2.5 select_add_fusion.2
  333.2 3.0 fusion.33
  336.1 2.5 select_add_fusion.2
  338.6 3.0 fusion.33
  341.6 2.5 select_add_fusion.2
  344.1 0.3 convert_element_type.33
  344.4 2.4 copy.27
  (19 shorter events, 0.1 us)
Async XLA Ops:
  7.4 200.3 %all-gather.5.cloned.1.call-start = ((), (), s32[]{:S(2)}) async-start(), calls=%async_computation.1 | async-start | bytes 5406720 | tf_op jit(solution)/shard_map/all_gather | solution.py:134
  8.1 19.1 %collective-permute-start = (bf16[60,128]{1,0:T(8,128)(2,1)S(1)}, bf16[60,128]{1,0:T(8,128)(2,1)S(1)}, u32[]{:S(2)}, u32[]{:S(2)}) collective-permute-start(bf16[60,128]{1,0:T(8,128)(2,1)S(1)} %slice.33), channel_id=1, source_target_pairs={{0,32},{32,64},{64,96},{96,128},{128,160},{160,192},{192,224},{1,3... | collective-permute-start | bytes 46088 | tf_op jit(solution)/shard_map/ppermute | solution.py:19
  14.4 12.8 %copy-start.3 = (bf16[500,60,1]{0,1,2:T(8,128)(2,1)S(1)}, bf16[500,60,1]{0,1,2:T(8,128)(2,1)}, u32[]{:S(2)}) copy-start(bf16[500,60,1]{0,1,2:T(8,128)(2,1)} %constant.103) | copy-start | bytes 180004
  27.2 3.0 copy-start.2
  30.2 7.5 %copy-start = (f32[16,128,500]{1,2,0:T(8,128)}, f32[16,128,500]{1,2,0:T(8,128)S(1)}, u32[]{:S(2)}) copy-start(f32[16,128,500]{1,2,0:T(8,128)S(1)} %bitcast_add_fusion.1) | copy-start | bytes 12288004
  30.2 9.4 %copy-start.5 = (f32[17,16]{1,0:T(8,128)S(1)}, f32[17,16]{1,0:T(8,128)}, u32[]{:S(2)}) copy-start(f32[17,16]{1,0:T(8,128)} %constant.98.clone) | copy-start | bytes 3268
  30.2 21.0 %copy-start.8 = (f32[16]{0:T(128)S(1)}, f32[16]{0:T(128)}, u32[]{:S(2)}) copy-start(f32[16]{0:T(128)} %constant.99.clone) | copy-start | bytes 196
  30.2 21.1 %copy-start.4 = (bf16[40,500,1]{1,0,2:T(8,128)(2,1)S(1)}, bf16[40,500,1]{1,0,2:T(8,128)(2,1)}, u32[]{:S(2)}) copy-start(bf16[40,500,1]{1,0,2:T(8,128)(2,1)} %constant.105) | copy-start | bytes 120004
  30.3 21.1 %copy-start.7 = (f32[500]{0:T(512)S(1)}, f32[500]{0:T(512)}, u32[]{:S(2)}) copy-start(f32[500]{0:T(512)} %constant.100.clone) | copy-start | bytes 6004
  37.7 2.0 copy-start.1
  51.4 5.3 %copy-start.6 = (s32[2]{0:T(128)S(1)}, s32[2]{0:T(128)}, u32[]{:S(2)}) copy-start(s32[2]{0:T(128)} %param.15) | copy-start | bytes 28
  216.3 77.7 %all-to-all-start = ((bf16[8,1,16,40,160]{4,3,2,1,0:T(8,128)(2,1)}), bf16[8,1,16,40,160]{4,3,2,1,0:T(8,128)(2,1)}, u32[]{:S(2)}, u32[]{:S(2)}) async-start(bf16[8,1,16,40,160]{4,3,2,1,0:T(8,128)(2,1)} %fusion.7), calls=%async_computation | async-start | bytes 5242880 | tf_op jit(solution)/shard_map/all_to_all | solution.py:139
  222.1 50.8 %all-gather.7.cloned.1.call-start = ((), (), s32[]{:S(2)}) async-start(), calls=%async_computation.2 | async-start | bytes 1474560 | tf_op jit(solution)/shard_map/all_gather | solution.py:88
Sparse Core Ops, SparseCore 0:
  56.7 150.9 all-gather.4
Sparse Core Ops, SparseCore 1:
  224.3 48.5 all-gather.6
